TPU v7x, 32 devices: a whole 2x2x4 slice. The times are simulated.
32 devices in a mesh: dp: 2 (over y), head: 4 (over z), tensor: 4 (over x, core).
Axes of the slice: x: 2, y: 2, z: 4, core: 2. Of those that a mesh axis runs over, the one named last changes fastest.
Arguments:
- tokens: bfloat16 [512, 8192], P('dp', 'tensor'), may hold values from -6 to 6
- cotangent: bfloat16 [512, 8192], P('dp', 'tensor'), may hold values from -6 to 6
- w_gate: bfloat16 [8192, 29568], P('tensor', 'head'), may hold values from -0.0625 to 0.0625
- w_up: bfloat16 [8192, 29568], P('tensor', 'head'), may hold values from -0.0625 to 0.0625
- w_down: bfloat16 [29568, 8192], P('head', 'tensor'), may hold values from -0.03125 to 0.03125
- common_down_factor: bfloat16 [8192, 64], P('tensor'), may hold values from -0.0625 to 0.0625
- head_up: bfloat16 [64, 64, 8192], P('head', None, 'tensor'), may hold values from -0.0625 to 0.0625
- routes: int32 [512, 1], P('dp'), may hold values from 0 to 63
Outputs:
- grad_x: bfloat16 [512, 8192], P(('dp', 'head'), 'tensor')
- grad_shared: float32 [8192, 64], P('tensor')
- up_head_gradients: float32 [64, 64, 8192], P('head', None, 'tensor')
Inputs may be any that keep to these rules, and one draw needn't show every extreme that they name: `routes`: each token names one adapter head; the loads are skewed.
All inputs are finite; a program needn't handle non-finite values.
Results may differ from a plain program's by a relative error of at most 0.015.
Values may be sent and summed in bfloat16 or wider, within the bound.
No kernel may reach another device: no remote copies, remote signals or barrier semaphores. Data moves between devices by JAX's collectives and lax.ppermute only.
A program may use at most 256 MiB of HBM per device.

v0:
```python
import jax
import jax.numpy as jnp
from jax import lax
from jax.sharding import PartitionSpec as P

ADAPTER_SCALE = 2.0


def contract_last(left, right):
    return lax.dot_general(
        left, right, (((1,), (1,)), ((), ())), preferred_element_type=jnp.float32
    )


def local(tokens, cotangent, w_gate, w_up, w_down, common_down_factor, head_up, routes):
    tok_rows, d_cols = tokens.shape
    hidden_activation = w_gate.shape[1]
    reduced_activation = common_down_factor.shape[1]
    local_heads = head_up.shape[0]
    first_head = lax.axis_index("head") * local_heads
    assigned_mask = (
        routes == first_head + jnp.arange(local_heads, dtype=jnp.int32)[None, :]
    ).astype(jnp.float32)
    flat_heads = head_up.reshape(local_heads * reduced_activation, d_cols)
    gate_preactivation = jnp.dot(tokens, w_gate, preferred_element_type=jnp.float32)
    up_preactivation = jnp.dot(tokens, w_up, preferred_element_type=jnp.float32)
    returned_gradient = contract_last(cotangent, w_down)
    adapter_selectors = jnp.dot(tokens, common_down_factor, preferred_element_type=jnp.float32)
    head_separated = contract_last(cotangent, flat_heads).reshape(
        tok_rows // lax.axis_size("tensor") * lax.axis_size("tensor"),
        local_heads,
        reduced_activation,
    )
    selector_gradient = ADAPTER_SCALE * jnp.sum(head_separated * assigned_mask[:, :, None], axis=1)
    shared_rows = lax.psum_scatter(
        jnp.concatenate(
            [
                gate_preactivation,
                up_preactivation,
                returned_gradient,
                adapter_selectors,
                selector_gradient,
            ],
            axis=1,
        ),
        "tensor",
        scatter_dimension=0,
        tiled=True,
    )
    gate_preactivation = shared_rows[:, :hidden_activation]
    up_preactivation = shared_rows[:, hidden_activation : 2 * hidden_activation]
    returned_gradient = shared_rows[:, 2 * hidden_activation : 3 * hidden_activation]
    adapter_selectors = shared_rows[
        :, 3 * hidden_activation : 3 * hidden_activation + reduced_activation
    ].astype(jnp.bfloat16)
    selector_gradient = shared_rows[:, 3 * hidden_activation + reduced_activation :].astype(
        jnp.bfloat16
    )
    sig_gate = jax.nn.sigmoid(gate_preactivation)
    gate_gradient = (
        returned_gradient
        * up_preactivation
        * sig_gate
        * (1.0 + gate_preactivation * (1.0 - sig_gate))
    ).astype(jnp.bfloat16)
    up_gradient = (returned_gradient * gate_preactivation * sig_gate).astype(jnp.bfloat16)
    gate_gradient, up_gradient, adapter_selectors, selector_gradient = (
        gate_gradient,
        up_gradient,
        adapter_selectors,
        selector_gradient,
    )
    packed = jnp.concatenate(
        [gate_gradient, up_gradient, adapter_selectors, selector_gradient], axis=1
    )
    part_rows = lax.all_gather(packed, "tensor", axis=0, tiled=True)
    ffn_rows = contract_last(part_rows[:, :hidden_activation], w_gate) + contract_last(
        part_rows[:, hidden_activation : 2 * hidden_activation], w_up
    )
    gathered = jnp.concatenate(
        [ffn_rows, part_rows[:, 2 * hidden_activation :].astype(jnp.float32)], axis=1
    )
    ffn_part = gathered[:, :d_cols]
    adapter_selectors = gathered[:, d_cols : d_cols + reduced_activation].astype(jnp.bfloat16)
    selector_gradient = gathered[:, d_cols + reduced_activation :].astype(jnp.bfloat16)
    own_ffn, own_code = (
        lax.psum_scatter(ffn_part, "head", scatter_dimension=0, tiled=True),
        lax.psum_scatter(
            selector_gradient.astype(jnp.float32), "head", scatter_dimension=0, tiled=True
        ),
    )
    grad_x = (own_ffn + contract_last(own_code.astype(jnp.bfloat16), common_down_factor)).astype(
        jnp.bfloat16
    )
    selector_mask = (
        adapter_selectors[:, None, :] * assigned_mask[:, :, None].astype(jnp.bfloat16)
    ).reshape(tok_rows, local_heads * reduced_activation)
    head_contributions = ADAPTER_SCALE * lax.dot_general(
        selector_mask, cotangent, (((0,), (0,)), ((), ())), preferred_element_type=jnp.float32
    )
    up_head_gradients = lax.psum(
        head_contributions.reshape(local_heads, reduced_activation, d_cols).astype(jnp.bfloat16),
        "dp",
    ).astype(jnp.float32)
    shared_term = lax.dot_general(
        tokens, selector_gradient, (((0,), (0,)), ((), ())), preferred_element_type=jnp.float32
    )
    grad_shared = lax.psum(shared_term.astype(jnp.bfloat16), ("dp", "head")).astype(jnp.float32)
    return (grad_x, grad_shared, up_head_gradients)


def solution(mesh):
    placed = (
        P("dp", "tensor"),
        P("dp", "tensor"),
        P("tensor", "head"),
        P("tensor", "head"),
        P("head", "tensor"),
        P("tensor", None),
        P("head", None, "tensor"),
        P("dp", None),
    )
    return jax.shard_map(
        local,
        mesh=mesh,
        in_specs=placed,
        out_specs=(P(("dp", "head"), "tensor"), P("tensor", None), P("head", None, "tensor")),
        check_vma=False,
    )
```

profile of v0, /device:TPU:0, one launch (start us, length us, event | category | flops | bytes accessed | tf_op | source)
XLA Modules:
  0.0 568.6 jit_solution(10104915546490771158)
XLA Ops:
  7.2 0.8 fusion.15
  8.4 15.7 %convolution_dynamic-update-slice_fusion.2 = f32[256,22304]{0,1:T(8,128)} fusion(bf16[256,2048]{1,0:T(8,128)(2,1)S(1)} %copy-done, bf16[2048,7392]{0,1:T(8,128)(2,1)} %param.10), kind=kOutput, calls=%fused_computation.2 | convolution fusion | flops 7751073792 | bytes 38895616 | tf_op jit(solution)/shard_map/dot_general | solution.py:25
  24.1 15.9 %convolution_dynamic-update-slice_fusion.1 = f32[256,22304]{0,1:T(8,128)} fusion(f32[256,22304]{0,1:T(8,128)} %convolution_dynamic-update-slice_fusion.2, bf16[256,2048]{1,0:T(8,128)(2,1)S(1)} %copy-done, bf16[2048,7392]{0,1:T(8,128)(2,1)} %param.11), kind=kOutput, calls=%fused_computation.1 | convolution fusion | flops 7751073792 | bytes 38895616 | tf_op jit(solution)/shard_map/dot_general | solution.py:26
  40.0 1.3 fusion.12
  41.3 15.8 %convolution_dynamic-update-slice_fusion = f32[256,22304]{0,1:T(8,128)} fusion(f32[256,22304]{0,1:T(8,128)} %convolution_dynamic-update-slice_fusion.1, bf16[256,2048]{1,0:T(8,128)(2,1)S(1)} %copy-done.3, bf16[7392,2048]{1,0:T(8,128)(2,1)} %param.12), kind=kOutput, calls=%fused_computation | convolution fusion | flops 7751073792 | bytes 38895616 | tf_op jit(solution)/shard_map/dot_general | solution.py:10
  57.1 1.1 convolution_dynamic-update-slice_fusion.3
  58.8 23.2 %copy.22 = f32[256,22304]{1,0:T(8,128)} copy(f32[256,22304]{0,1:T(8,128)} %multiply_dynamic-update-slice_fusion) | data formatting | bytes 45678592
  82.1 165.1 %reduce-scatter.10.cloned.1.call-done = f32[64,22304]{1,0:T(8,128)} async-done(((f32[256,22304]{1,0:T(8,128)}), f32[64,22304]{1,0:T(8,128)}) %reduce-scatter.10.cloned.1.call-update) | async-done | bytes 5709840 | tf_op jit(solution)/shard_map/reduce_scatter | solution.py:35
  247.2 0.9 slice.72
  248.1 3.7 multiply_convert_fusion.1
  251.9 2.4 concatenate.7
  254.3 54.3 %all-gather.2.cloned.1.call-done = bf16[256,14912]{1,0:T(8,128)(2,1)} async-done(((bf16[64,14912]{1,0:T(8,128)(2,1)}), bf16[256,14912]{1,0:T(8,128)(2,1)}) %all-gather.2.cloned.1.call-update) | async-done | bytes 7634960 | tf_op jit(solution)/shard_map/all_gather | solution.py:76
  308.6 1.0 fusion.17
  310.6 1.9 fusion.8
  312.6 4.5 multiply_convert_fusion
  317.2 15.2 %fusion = f32[256,2048]{1,0:T(8,128)S(1)} fusion(bf16[2048,7392]{0,1:T(8,128)(2,1)} %param.11, bf16[256,14912]{1,0:T(8,128)(2,1)} %all-gather.2.cloned.1.call-done), kind=kOutput, calls=%fused_computation.4 | convolution fusion | flops 7751073792 | bytes 36175872 | tf_op jit(solution)/shard_map/dot_general | solution.py:10
  332.3 15.9 %fusion.4 = f32[256,2048]{1,0:T(8,128)} fusion(f32[256,2048]{1,0:T(8,128)S(1)} %fusion, bf16[2048,7392]{0,1:T(8,128)(2,1)} %param.10, bf16[256,14912]{1,0:T(8,128)(2,1)} %all-gather.2.cloned.1.call-done), kind=kOutput, calls=%fused_computation.8 | convolution fusion | flops 7751598080 | bytes 38273024 | tf_op jit(solution)/shard_map/dot_general | solution.py:10
  348.3 0.8 copy.25
  349.1 54.8 %all-reduce.3.cloned.1.call-done = bf16[2048,64]{0,1:T(8,128)(2,1)} async-done(((bf16[2048,64]{0,1:T(8,128)(2,1)}), bf16[2048,64]{0,1:T(8,128)(2,1)}) %all-reduce.3.cloned.1.call-update) | async-done | bytes 262160 | tf_op jit(solution)/shard_map/psum | solution.py:108
  403.9 1.8 convert_element_type.64
  405.7 108.2 %all-reduce.5.cloned.1.call-done = bf16[16,64,2048]{2,1,0:T(8,128)(2,1)} async-done(((bf16[16,64,2048]{2,1,0:T(8,128)(2,1)}), bf16[16,64,2048]{2,1,0:T(8,128)(2,1)}) %all-reduce.5.cloned.1.call-update) | async-done | bytes 4194320 | tf_op jit(solution)/shard_map/psum | solution.py:101
  513.9 6.7 %convert_element_type.68 = f32[16,64,2048]{2,1,0:T(8,128)} convert(bf16[16,64,2048]{2,1,0:T(8,128)(2,1)} %all-reduce.5.cloned.1.call-done) | non-fusion elementwise | flops 2097152 | bytes 12582912 | tf_op jit(solution)/shard_map/convert_element_type | solution.py:104
  520.6 39.2 %reduce-scatter.8.cloned.1.call-done = f32[64,2048]{1,0:T(8,128)} async-done(((f32[256,2048]{1,0:T(8,128)}), f32[64,2048]{1,0:T(8,128)}) %reduce-scatter.8.cloned.1.call-update) | async-done | bytes 524304 | tf_op jit(solution)/shard_map/reduce_scatter | solution.py:87
  559.7 2.0 fusion.7
  (27 shorter events, 2.3 us)
Async XLA Ops:
  7.2 1.2 copy-start
  7.2 240.0 %reduce-scatter.10.cloned.1.call-start = ((), (), s32[]{:S(2)}) async-start(), calls=%async_computation.7 | async-start | bytes 28672000 | tf_op jit(solution)/shard_map/reduce_scatter | solution.py:35
  24.1 15.9 %copy-start.2 = (bf16[16,64,2048]{2,1,0:T(8,128)(2,1)S(1)}, bf16[16,64,2048]{2,1,0:T(8,128)(2,1)}, u32[]{:S(2)}) copy-start(bf16[16,64,2048]{2,1,0:T(8,128)(2,1)} %param.14) | copy-start | bytes 12582916
  24.1 15.9 %copy-start.3 = (bf16[256,2048]{1,0:T(8,128)(2,1)S(1)}, bf16[256,2048]{1,0:T(8,128)(2,1)}, u32[]{:S(2)}) copy-start(bf16[256,2048]{1,0:T(8,128)(2,1)} %param.9) | copy-start | bytes 3145732
  41.3 15.8 %copy-start.1 = (bf16[2048,64]{0,1:T(8,128)(2,1)S(1)}, bf16[2048,64]{0,1:T(8,128)(2,1)}, u32[]{:S(2)}) copy-start(bf16[2048,64]{0,1:T(8,128)(2,1)} %param.13) | copy-start | bytes 786436
  82.1 226.5 %all-gather.2.cloned.1.call-start = ((), (), s32[]{:S(2)}) async-start(), calls=%async_computation.3 | async-start | bytes 9584640 | tf_op jit(solution)/shard_map/all_gather | solution.py:76
  254.3 94.0 %reduce-scatter.12.cloned.1.call-start = ((), (), s32[]{:S(2)}) async-start(), calls=%async_computation.8 | async-start | bytes 163840
  310.5 93.3 %all-reduce.3.cloned.1.call-start = ((), (), s32[]{:S(2)}) async-start(), calls=%async_computation.5 | async-start | bytes 524288 | tf_op jit(solution)/shard_map/psum | solution.py:108
  312.5 201.4 %all-reduce.5.cloned.1.call-start = ((), (), s32[]{:S(2)}) async-start(), calls=%async_computation.6 | async-start | bytes 8388608 | tf_op jit(solution)/shard_map/psum | solution.py:101
  317.1 242.6 %reduce-scatter.8.cloned.1.call-start = ((), (), s32[]{:S(2)}) async-start(), calls=%async_computation.4 | async-start | bytes 2621440 | tf_op jit(solution)/shard_map/reduce_scatter | solution.py:87
Sparse Core Ops, SparseCore 0:
  82.2 164.9 reduce-scatter.9
  254.4 54.1 all-gather.1
  311.4 19.4 reduce-scatter.11
  334.7 69.1 all-reduce.2
  406.7 107.1 all-reduce.4
  516.0 43.6 reduce-scatter.7
where the time goes:
time: 569 us
  waiting for transfers between devices  422 us (74%)
  matrix products  89.2 us (16%)
  local copies, waits for them, and re-layouts  29.6 us (5%)
  between operations  14.2 us (2%)
  other arithmetic  13.7 us (2%)
    reduce_scatter x1, waiting for transfers between devices, local(): lax.psum_scatter(jnp.concatenate([gate_preactivation, up_preactivation, r...  165 us
    psum x1, waiting for transfers between devices, local(): lax.psum(head_contributions.reshape(local_heads, reduced_activation, d_co...  108 us
    psum x1, waiting for transfers between devices, local(): lax.psum(shared_term.astype(jnp.bfloat16), ('dp', 'head'))  54.8 us
    all_gather x1, waiting for transfers between devices, local(): part_rows = lax.all_gather(packed, 'tensor', axis=0, tiled=True)  54.3 us
    dot_general x5, matrix products, contract_last(): lax.dot_general(left, right, (((1,), (1,)), ((), ())), preferred_element_...  50.1 us
    reduce_scatter x1, waiting for transfers between devices, local(): lax.psum_scatter(ffn_part, 'head', scatter_dimension=0, tiled=True)  39.2 us
    unnamed x12, local copies, waits for them, and re-layouts  25.3 us
    dot_general x1, matrix products, local(): up_preactivation = jnp.dot(tokens, w_up, preferred_element_type=jnp.float32)  15.9 us
  transfers between devices with their start and end apart: 6, of which 5 were waited for; matrix products, arithmetic and copies ran while one was open for 8% of the time, Pallas kernels for 0%

commit v1 on v0

--- a/solution.py
+++ b/solution.py
@@ -105,7 +105,9 @@
     shared_term = lax.dot_general(
         tokens, selector_gradient, (((0,), (0,)), ((), ())), preferred_element_type=jnp.float32
     )
-    grad_shared = lax.psum(shared_term.astype(jnp.bfloat16), ("dp", "head")).astype(jnp.float32)
+    grad_shared = jnp.sum(
+        lax.all_gather(shared_term.astype(jnp.bfloat16), ("dp", "head")), axis=0
+    ).astype(jnp.float32)
     return (grad_x, grad_shared, up_head_gradients)
 
 

time: 569 us -> 546 us (0.960)
  waiting for transfers between devices: 422 us -> 394 us
    psum x1 -> x0, waiting for transfers between devices: 54.8 us -> none  [local(): lax.psum(shared_term.astype(jnp.bfloat16), ('dp', 'head'))]
    all_gather x0 -> x1, waiting for transfers between devices: none -> 31.5 us  [local(): lax.all_gather(shared_term.astype(jnp.bfloat16), ('dp', 'head'))]
    unnamed x12 -> x13, local copies, waits for them, and re-layouts: 25.3 us -> 28 us
  transfers between devices with their start and end apart: 6 -> 6, of which waited for: 5 -> 5; matrix products, arithmetic and copies ran while one was open for 8% -> 9% of each run, Pallas kernels for 0% -> 0%
where the time goes in v1:
time: 546 us; the launch traced here: 545 us
  waiting for transfers between devices  394 us (72%)
  matrix products  89.4 us (16%)
  local copies, waits for them, and re-layouts  32.4 us (6%)
  other arithmetic  14.3 us (3%)
  between operations  14.2 us (3%)
    reduce_scatter x1, waiting for transfers between devices, local(): lax.psum_scatter(jnp.concatenate([gate_preactivation, up_preactivation, r...  165 us
    psum x1, waiting for transfers between devices, local(): lax.psum(head_contributions.reshape(local_heads, reduced_activation, d_co...  104 us
    all_gather x1, waiting for transfers between devices, local(): part_rows = lax.all_gather(packed, 'tensor', axis=0, tiled=True)  54.3 us
    dot_general x5, matrix products, contract_last(): lax.dot_general(left, right, (((1,), (1,)), ((), ())), preferred_element_...  50.3 us
    reduce_scatter x1, waiting for transfers between devices, local(): lax.psum_scatter(ffn_part, 'head', scatter_dimension=0, tiled=True)  39.2 us
    all_gather x1, waiting for transfers between devices, local(): lax.all_gather(shared_term.astype(jnp.bfloat16), ('dp', 'head'))  31.5 us
    unnamed x13, local copies, waits for them, and re-layouts  28 us
    dot_general x1, matrix products, local(): up_preactivation = jnp.dot(tokens, w_up, preferred_element_type=jnp.float32)  15.9 us
  transfers between devices with their start and end apart: 6, of which 5 were waited for; matrix products, arithmetic and copies ran while one was open for 9% of the time, Pallas kernels for 0%

profile of v1, /device:TPU:0, one launch (start us, length us, event | category | flops | bytes accessed | tf_op | source)
XLA Modules:
  0.0 544.8 jit_solution(9775679217820932028)
XLA Ops:
  8.4 15.7 %convolution_dynamic-update-slice_fusion.2 = f32[256,22304]{0,1:T(8,128)} fusion(bf16[256,2048]{1,0:T(8,128)(2,1)S(1)} %copy-done, bf16[2048,7392]{0,1:T(8,128)(2,1)} %param.10), kind=kOutput, calls=%fused_computation.2 | convolution fusion | flops 7751073792 | bytes 38895616 | tf_op jit(solution)/shard_map/dot_general | solution.py:25
  24.1 15.9 %convolution_dynamic-update-slice_fusion.1 = f32[256,22304]{0,1:T(8,128)} fusion(f32[256,22304]{0,1:T(8,128)} %convolution_dynamic-update-slice_fusion.2, bf16[256,2048]{1,0:T(8,128)(2,1)S(1)} %copy-done, bf16[2048,7392]{0,1:T(8,128)(2,1)} %param.11), kind=kOutput, calls=%fused_computation.1 | convolution fusion | flops 7751073792 | bytes 38895616 | tf_op jit(solution)/shard_map/dot_general | solution.py:26
  40.0 1.3 fusion.12
  41.3 15.8 %convolution_dynamic-update-slice_fusion = f32[256,22304]{0,1:T(8,128)} fusion(f32[256,22304]{0,1:T(8,128)} %convolution_dynamic-update-slice_fusion.1, bf16[256,2048]{1,0:T(8,128)(2,1)S(1)} %copy-done.3, bf16[7392,2048]{1,0:T(8,128)(2,1)} %param.12), kind=kOutput, calls=%fused_computation | convolution fusion | flops 7751073792 | bytes 38895616 | tf_op jit(solution)/shard_map/dot_general | solution.py:10
  57.1 1.1 convolution_dynamic-update-slice_fusion.3
  58.8 23.2 %copy.22 = f32[256,22304]{1,0:T(8,128)} copy(f32[256,22304]{0,1:T(8,128)} %multiply_dynamic-update-slice_fusion) | data formatting | bytes 45678592
  82.1 165.1 %reduce-scatter.10.cloned.1.call-done = f32[64,22304]{1,0:T(8,128)} async-done(((f32[256,22304]{1,0:T(8,128)}), f32[64,22304]{1,0:T(8,128)}) %reduce-scatter.10.cloned.1.call-update) | async-done | bytes 5709840 | tf_op jit(solution)/shard_map/reduce_scatter | solution.py:35
  247.2 0.9 slice.72
  248.1 3.7 multiply_convert_fusion.1
  251.9 2.4 concatenate.7
  254.3 54.3 %all-gather.4.cloned.1.call-done = bf16[256,14912]{1,0:T(8,128)(2,1)} async-done(((bf16[64,14912]{1,0:T(8,128)(2,1)}), bf16[256,14912]{1,0:T(8,128)(2,1)}) %all-gather.4.cloned.1.call-update) | async-done | bytes 7634960 | tf_op jit(solution)/shard_map/all_gather | solution.py:76
  308.6 1.0 fusion.17
  310.5 1.9 fusion.8
  312.6 4.5 multiply_convert_fusion
  317.2 15.2 %fusion = f32[256,2048]{1,0:T(8,128)S(1)} fusion(bf16[2048,7392]{0,1:T(8,128)(2,1)} %param.11, bf16[256,14912]{1,0:T(8,128)(2,1)} %all-gather.4.cloned.1.call-done), kind=kOutput, calls=%fused_computation.4 | convolution fusion | flops 7751073792 | bytes 36175872 | tf_op jit(solution)/shard_map/dot_general | solution.py:10
  332.3 16.1 %fusion.4 = f32[256,2048]{1,0:T(8,128)} fusion(f32[256,2048]{1,0:T(8,128)S(1)} %fusion, bf16[2048,7392]{0,1:T(8,128)(2,1)} %param.10, bf16[256,14912]{1,0:T(8,128)(2,1)} %all-gather.4.cloned.1.call-done), kind=kOutput, calls=%fused_computation.8 | convolution fusion | flops 7751598080 | bytes 38273024 | tf_op jit(solution)/shard_map/dot_general | solution.py:10
  348.4 0.8 copy.25
  349.3 31.5 %all-gather.6.cloned.1.call-done = bf16[16384,64]{0,1:T(8,128)(2,1)} async-done(((bf16[2048,64]{0,1:T(8,128)(2,1)}), bf16[16384,64]{0,1:T(8,128)(2,1)}) %all-gather.6.cloned.1.call-update) | async-done | bytes 2097168 | tf_op jit(solution)/shard_map/all_gather | solution.py:109
  380.8 2.8 copy.27
  383.6 1.6 bitcast_reduce_fusion
  386.0 104.2 %all-reduce.2.cloned.1.call-done = bf16[16,64,2048]{2,1,0:T(8,128)(2,1)} async-done(((bf16[16,64,2048]{2,1,0:T(8,128)(2,1)}), bf16[16,64,2048]{2,1,0:T(8,128)(2,1)}) %all-reduce.2.cloned.1.call-update) | async-done | bytes 4194320 | tf_op jit(solution)/shard_map/psum | solution.py:101
  490.1 6.7 %convert_element_type.70 = f32[16,64,2048]{2,1,0:T(8,128)} convert(bf16[16,64,2048]{2,1,0:T(8,128)(2,1)} %all-reduce.2.cloned.1.call-done) | non-fusion elementwise | flops 2097152 | bytes 12582912 | tf_op jit(solution)/shard_map/convert_element_type | solution.py:104
  496.8 39.2 %reduce-scatter.8.cloned.1.call-done = f32[64,2048]{1,0:T(8,128)} async-done(((f32[256,2048]{1,0:T(8,128)}), f32[64,2048]{1,0:T(8,128)}) %reduce-scatter.8.cloned.1.call-update) | async-done | bytes 524304 | tf_op jit(solution)/shard_map/reduce_scatter | solution.py:87
  535.9 2.0 fusion.7
  (29 shorter events, 4.0 us)
Async XLA Ops:
  7.2 1.2 copy-start
  7.2 240.0 %reduce-scatter.10.cloned.1.call-start = ((), (), s32[]{:S(2)}) async-start(), calls=%async_computation.7 | async-start | bytes 28672000 | tf_op jit(solution)/shard_map/reduce_scatter | solution.py:35
  24.1 15.9 %copy-start.2 = (bf16[16,64,2048]{2,1,0:T(8,128)(2,1)S(1)}, bf16[16,64,2048]{2,1,0:T(8,128)(2,1)}, u32[]{:S(2)}) copy-start(bf16[16,64,2048]{2,1,0:T(8,128)(2,1)} %param.14) | copy-start | bytes 12582916
  24.1 15.9 %copy-start.3 = (bf16[256,2048]{1,0:T(8,128)(2,1)S(1)}, bf16[256,2048]{1,0:T(8,128)(2,1)}, u32[]{:S(2)}) copy-start(bf16[256,2048]{1,0:T(8,128)(2,1)} %param.9) | copy-start | bytes 3145732
  41.3 15.8 %copy-start.1 = (bf16[2048,64]{0,1:T(8,128)(2,1)S(1)}, bf16[2048,64]{0,1:T(8,128)(2,1)}, u32[]{:S(2)}) copy-start(bf16[2048,64]{0,1:T(8,128)(2,1)} %param.13) | copy-start | bytes 786436
  82.1 226.5 %all-gather.4.cloned.1.call-start = ((), (), s32[]{:S(2)}) async-start(), calls=%async_computation.3 | async-start | bytes 9584640 | tf_op jit(solution)/shard_map/all_gather | solution.py:76
  254.3 94.2 %reduce-scatter.12.cloned.1.call-start = ((), (), s32[]{:S(2)}) async-start(), calls=%async_computation.8 | async-start | bytes 163840
  310.4 70.3 %all-gather.6.cloned.1.call-start = ((), (), s32[]{:S(2)}) async-start(), calls=%async_computation.6 | async-start | bytes 2359296 | tf_op jit(solution)/shard_map/all_gather | solution.py:109
  312.4 177.7 %all-reduce.2.cloned.1.call-start = ((), (), s32[]{:S(2)}) async-start(), calls=%async_computation.5 | async-start | bytes 8388608 | tf_op jit(solution)/shard_map/psum | solution.py:101
  317.1 218.8 %reduce-scatter.8.cloned.1.call-start = ((), (), s32[]{:S(2)}) async-start(), calls=%async_computation.4 | async-start | bytes 2621440 | tf_op jit(solution)/shard_map/reduce_scatter | solution.py:87
Sparse Core Ops, SparseCore 0:
  82.2 164.9 reduce-scatter.9
  254.4 54.1 all-gather.3
  311.4 19.4 reduce-scatter.11
  333.5 47.2 all-gather.5
  383.6 106.4 all-reduce.1
  492.3 43.6 reduce-scatter.7
